TPU v7x, 128 devices: a whole 4x4x4 slice. The times are simulated.
128 devices in a mesh: ctx: 16 (over y, z_hi, core), head: 8 (over x, z_lo).
Axes of the slice: x: 4, y: 4, z: 4 (z_hi: 2, z_lo: 2; z = z_hi * 2 + z_lo), core: 2. Of those that a mesh axis runs over, the one named last changes fastest.
Arguments:
- queries: bfloat16 [2048, 12288], P('ctx', 'head'), may hold values from -8 to 8
- latents: bfloat16 [2048, 512], P('ctx'), may hold values from -4 to 4
- rope_key: bfloat16 [2048, 64], P('ctx'), may hold values from -8 to 8
- up_key_weight: bfloat16 [512, 8192], P(None, 'head'), may hold values from -0.5 to 0.5
- up_value_weight: bfloat16 [512, 8192], P(None, 'head'), may hold values from -0.25 to 0.25
- out_grad: bfloat16 [2048, 8192], P('ctx', 'head'), may hold values from -6 to 6
- group_order: int32 [32], replicated, may hold values from 0 to 31, as said below
Outputs:
- query_grad: bfloat16 [2048, 12288], P('ctx', 'head')
- latent_grad: float32 [2048, 512], P('ctx')
- rope_grad: float32 [2048, 64], P('ctx')
- up_key_grad: float32 [512, 8192], P('ctx', 'head')
- up_value_grad: float32 [512, 8192], P('ctx', 'head')
Inputs may be any that keep to these rules, and one draw needn't show every extreme that they name: A permutation of the 32 group numbers; storage slot k (rows k * 64 to k * 64 + 63) holds the sequence positions group_order[k] * 64 on, in order.
All inputs are finite; a program needn't handle non-finite values.
Results may differ from a plain program's by a relative error of at most 0.017.
Values may be sent and summed in bfloat16 or wider, within the bound.
No kernel may reach another device: no remote copies, remote signals or barrier semaphores. Data moves between devices by JAX's collectives and lax.ppermute only.
A program may use at most 64 MiB of HBM per device.

v0:
```python
import jax
import jax.numpy as jnp
from jax import lax
from jax.sharding import PartitionSpec as P

D_LATENT = 512
ROPE = 64
NOPE = 128
VDIM = 128
NEG_FILL = -1e30


def product(pattern, left_side, right_side):
    return jnp.einsum(pattern, left_side, right_side, preferred_element_type=jnp.float32)


def token_positions(group_order, row_ids, group_len):
    slot_ids = row_ids // group_len
    slot_table = jnp.arange(group_order.shape[0], dtype=jnp.int32)
    picked = jnp.sum(
        jnp.where(slot_ids[:, None] == slot_table[None, :], group_order[None, :], 0), axis=1
    )
    return picked * group_len + row_ids % group_len


def per_device(queries, latents, rope_key, up_key_weight, up_value_weight, out_grad, group_order):
    tok_count = queries.shape[0]
    head_count = up_key_weight.shape[1] // NOPE
    group_len = tok_count // 2
    scale_factor = (NOPE + ROPE) ** (-0.5)
    shaped = queries.reshape(tok_count, head_count, NOPE + ROPE)
    query_nope = shaped[:, :, :NOPE]
    query_rope = shaped[:, :, NOPE:]
    up_key = up_key_weight.reshape(D_LATENT, head_count, NOPE)
    up_value = up_value_weight.reshape(D_LATENT, head_count, VDIM)
    grad_out = out_grad.reshape(tok_count, head_count, VDIM)
    query_abs = product("thd,khd->thk", query_nope, up_key).astype(jnp.bfloat16)
    grad_lat = product("thd,khd->thk", grad_out, up_value).astype(jnp.bfloat16)
    own_rows = lax.axis_index("ctx") * tok_count + jnp.arange(tok_count, dtype=jnp.int32)
    query_pos = token_positions(group_order, own_rows, group_len)

    def piece_scores(latent_piece, rope_piece):
        scores = product("thk,nk->thn", query_abs, latent_piece) + product(
            "thr,nr->thn", query_rope, rope_piece
        )
        return scores * scale_factor

    latent_piece = lax.all_gather(latents, "ctx", axis=0, tiled=True)
    rope_piece = lax.all_gather(rope_key, "ctx", axis=0, tiled=True)
    row_count = latent_piece.shape[0]
    key_pos = token_positions(group_order, jnp.arange(row_count, dtype=jnp.int32), group_len)
    visible = key_pos[None, None, :] <= query_pos[:, None, None]
    run_max = jnp.full((tok_count, head_count), NEG_FILL, jnp.float32)
    scores = piece_scores(latent_piece, rope_piece)
    grad_prob = product("thk,nk->thn", grad_lat, latent_piece)
    new_max = jnp.maximum(run_max, jnp.max(jnp.where(visible, scores, NEG_FILL), axis=2))
    weights = jnp.where(visible, jnp.exp(scores - new_max[:, :, None]), 0.0)
    forward_state = (new_max, jnp.sum(weights, axis=2), jnp.sum(weights * grad_prob, axis=2))
    run_max, run_sum, run_dot = forward_state
    log_total = run_max + jnp.log(run_sum)
    row_delta = run_dot / run_sum
    latent_piece = lax.all_gather(latents, "ctx", axis=0, tiled=True)
    rope_piece = lax.all_gather(rope_key, "ctx", axis=0, tiled=True)
    row_count = latent_piece.shape[0]
    key_pos = token_positions(group_order, jnp.arange(row_count, dtype=jnp.int32), group_len)
    visible = key_pos[None, None, :] <= query_pos[:, None, None]
    scores = piece_scores(latent_piece, rope_piece)
    softmax_rows = jnp.where(visible, jnp.exp(scores - log_total[:, :, None]), 0.0)
    grad_prob = product("thk,nk->thn", grad_lat, latent_piece)
    grad_score = softmax_rows * (grad_prob - row_delta[:, :, None]) * scale_factor
    probs_low = softmax_rows.astype(jnp.bfloat16)
    grad_low = grad_score.astype(jnp.bfloat16)
    acc_out = product("thn,nk->thk", probs_low, latent_piece)
    acc_query = product("thn,nk->thk", grad_low, latent_piece)
    acc_rope = product("thn,nr->thr", grad_low, rope_piece)
    latent_part = product("thn,thk->nk", grad_low, query_abs) + product(
        "thn,thk->nk", probs_low, grad_lat
    )
    rope_part = product("thn,thr->nr", grad_low, query_rope)
    all_latent = latent_part
    all_rope = rope_part
    backward_state = (acc_query, acc_rope, acc_out, all_latent, all_rope)
    acc_query, acc_rope, acc_out, all_latent, all_rope = backward_state
    grad_abs = acc_query.astype(jnp.bfloat16)
    grad_nope = product("thk,khd->thd", grad_abs, up_key)
    query_grad = (
        jnp.concatenate([grad_nope, acc_rope], axis=2).astype(jnp.bfloat16).reshape(tok_count, -1)
    )
    out_low = acc_out.astype(jnp.bfloat16)
    weight_key_grad = product("thk,thd->khd", grad_abs, query_nope).reshape(D_LATENT, -1)
    weight_value_grad = product("thk,thd->khd", out_low, grad_out).reshape(D_LATENT, -1)
    up_key_grad, up_value_grad = (
        lax.psum_scatter(
            weight_key_grad.astype(jnp.bfloat16), "ctx", scatter_dimension=0, tiled=True
        ).astype(jnp.float32),
        lax.psum_scatter(
            weight_value_grad.astype(jnp.bfloat16), "ctx", scatter_dimension=0, tiled=True
        ).astype(jnp.float32),
    )
    partial_latent, partial_rope = (
        lax.psum_scatter(
            all_latent.astype(jnp.bfloat16), "ctx", scatter_dimension=0, tiled=True
        ).astype(jnp.float32),
        lax.psum_scatter(
            all_rope.astype(jnp.bfloat16), "ctx", scatter_dimension=0, tiled=True
        ).astype(jnp.float32),
    )
    latent_grad, rope_grad = (
        lax.psum(partial_latent.astype(jnp.bfloat16), "head").astype(jnp.float32),
        lax.psum(partial_rope.astype(jnp.bfloat16), "head").astype(jnp.float32),
    )
    return (query_grad, latent_grad, rope_grad, up_key_grad, up_value_grad)


def solution(mesh):
    placed = (
        P("ctx", "head"),
        P("ctx", None),
        P("ctx", None),
        P(None, "head"),
        P(None, "head"),
        P("ctx", "head"),
        P(),
    )
    return jax.shard_map(
        per_device,
        mesh=mesh,
        in_specs=placed,
        out_specs=(
            P("ctx", "head"),
            P("ctx", None),
            P("ctx", None),
            P("ctx", "head"),
            P("ctx", "head"),
        ),
        check_vma=False,
    )
```

profile of v0, /device:TPU:0, one launch (start us, length us, event | category | flops | bytes accessed | tf_op | source)
XLA Modules:
  0.0 446.0 jit_solution(16935749232204141822)
XLA Ops:
  7.2 0.0 copy-start
  7.2 0.0 all-gather.2.cloned.1.call-start
  7.2 0.7 all-gather.2.cloned.1.call-update
  7.9 0.0 reduce-scatter.7.cloned.1.call-start
  8.0 1.2 copy.63
  9.2 1.5 copy.90
  10.7 1.1 copy.91
  11.8 0.7 select_reduce_fusion.2
  12.6 0.8 select_reduce_fusion.1
  13.4 26.6 %all_gather.9 = bf16[2048,64]{0,1:T(8,128)(2,1)S(1)} all-gather(bf16[128,64]{0,1:T(8,128)(2,1)} %param.9), channel_id=1, replica_groups=mesh['ctx'=16,'head'=8] {'ctx'}, dimensions={0}, use_global_device_ids=true | all-gather | bytes 278528 | tf_op jit(solution)/shard_map/all_gather | solution.py:63
  40.0 1.5 fusion.18
  41.5 0.0 copy-done
  41.5 1.5 fusion.19
  42.9 0.2 broadcast_compare_fusion
  43.2 18.1 %all-gather.2.cloned.1.call-done = bf16[2048,512]{1,0:T(8,128)(2,1)} async-done(((bf16[128,512]{1,0:T(8,128)(2,1)}), bf16[2048,512]{1,0:T(8,128)(2,1)}) %all-gather.2.cloned.1.call-update) | async-done | bytes 2097168 | tf_op jit(solution)/shard_map/all_gather | solution.py:62
  61.3 4.3 fusion.10
  65.6 0.0 copy-done.3
  65.6 0.0 copy-start.6
  65.6 0.0 copy-start.8
  65.6 2.2 select_reduce_fusion
  67.8 0.0 copy-start.2
  67.9 0.0 copy-done.6
  67.9 0.0 copy-done.8
  67.9 4.3 fusion
  72.2 0.0 copy-start.7
  72.2 3.2 multiply_convert_fusion
  75.5 0.0 copy-start.1
  75.5 2.0 copy-done.1
  77.4 0.0 copy-done.7
  77.4 2.4 fusion.46
  79.9 0.0 copy-done.2
  79.9 4.7 %fusion.2 = bf16[2048,512]{1,0:T(8,128)(2,1)} fusion(f32[2048,512,1]{1,0,2:T(8,128)S(1)} %fusion.46, bf16[128,8,512]{0,2,1:T(8,128)(2,1)S(1)} %copy-done.6, f32[128,8,2048]{2,0,1:T(8,128)S(1)} %get-tuple-element.30, f32[128,8]{0,1:T(8,128)S(1)} %get-tuple-element.27, pred[128,2048]{1,0:T(8,128)(4,1)S(1)} %broadcast_compare_fusion), kind=kOutput, calls=%fused_computation.9 | convolution fusion | flops 2155872256 | bytes 15994880 | tf_op jit(solution)/shard_map/thn,thk->nk/dot_general | solution.py:14
  84.5 0.0 reduce-scatter.7.cloned.1.call-update
  84.6 0.0 reduce-scatter.13.cloned.1.call-start
  84.6 3.0 fusion.3
  87.7 1.0 copy.87
  88.7 0.0 reduce-scatter.13.cloned.1.call-update
  88.7 0.0 reduce-scatter.11.cloned.1.call-start
  88.8 7.7 %convolution_convert_fusion.1 = bf16[8,512,128]{1,2,0:T(8,128)(2,1)} fusion(bf16[128,8,128]{0,2,1:T(8,128)(2,1)S(1)} %bitcast.81, bf16[2048,512]{1,0:T(8,128)(2,1)} %all-gather.2.cloned.1.call-done, f32[128,8,2048]{2,0,1:T(8,128)} %copy-done.2, f32[128,8]{0,1:T(8,128)S(1)} %get-tuple-element.27, pred[128,2048]{1,0:T(8,128)(4,1)S(1)} %broadcast_compare_fusion), kind=kOutput, calls=%fused_computation.21 | convolution fusion | flops 2289041408 | bytes 12062720 | tf_op jit(solution)/shard_map/thk,thd->khd/dot_general | solution.py:14
  96.5 2.3 copy.78
  98.8 0.0 reduce-scatter.11.cloned.1.call-update
  98.8 0.3 reduce-scatter.9.cloned.1.call-start
  99.1 5.4 %fusion.12 = bf16[128,8,512]{2,0,1:T(8,128)(2,1)S(1)} fusion(bf16[128,8,2048]{2,0,1:T(8,128)(2,1)} %copy-done.1, bf16[2048,512]{1,0:T(8,128)(2,1)} %all-gather.2.cloned.1.call-done), kind=kOutput, calls=%fused_computation.24 | convolution fusion | flops 2148007936 | bytes 7340032 | tf_op jit(solution)/shard_map/thn,nk->thk/dot_general | solution.py:14
  104.5 1.4 convolution_convert_fusion
  105.9 2.4 copy.76
  108.2 0.0 reduce-scatter.9.cloned.1.call-update
  108.2 0.0 all-reduce.2.cloned.1.call-start
  108.3 1.1 fusion.22
  109.4 0.0 copy-done.4
  109.4 3.6 convolution_convert_fusion.5
  113.1 41.4 %reduce-scatter.7.cloned.1.call-done = bf16[128,512]{1,0:T(8,128)(2,1)} async-done(((bf16[2048,512]{1,0:T(8,128)(2,1)}), bf16[128,512]{1,0:T(8,128)(2,1)}) %reduce-scatter.7.cloned.1.call-update) | async-done | bytes 131088 | tf_op jit(solution)/shard_map/reduce_scatter | solution.py:101
  154.5 0.0 all-reduce.2.cloned.1.call-update
  154.5 0.0 copy-done.5
  154.6 0.9 copy.79
  155.5 67.5 %reduce-scatter.13.cloned.1.call-done = bf16[128,64]{1,0:T(8,128)(2,1)} async-done(((bf16[2048,64]{1,0:T(8,128)(2,1)}), bf16[128,64]{1,0:T(8,128)(2,1)}) %reduce-scatter.13.cloned.1.call-update) | async-done | bytes 16400
  223.0 0.8 copy.88
  223.8 33.4 %psum.15 = bf16[128,64]{0,1:T(8,128)(2,1)S(1)} all-reduce(bf16[128,64]{0,1:T(8,128)(2,1)S(1)} %copy.88), channel_id=1, replica_groups=mesh['ctx'=16,'head'=8] {'head'}, use_global_device_ids=true, to_apply=%region_8.9 | all-reduce | flops 8192 | bytes 32768 | tf_op jit(solution)/shard_map/psum | solution.py:110
  257.2 0.6 convert_element_type.80
  257.9 34.8 %reduce-scatter.11.cloned.1.call-done = bf16[32,1024]{1,0:T(8,128)(2,1)} async-done(((bf16[512,1024]{1,0:T(8,128)(2,1)}), bf16[32,1024]{1,0:T(8,128)(2,1)}) %reduce-scatter.11.cloned.1.call-update) | async-done | bytes 65552 | tf_op jit(solution)/shard_map/reduce_scatter | solution.py:96
  292.7 1.5 convert_element_type.89
  294.2 68.2 %reduce-scatter.9.cloned.1.call-done = bf16[32,1024]{1,0:T(8,128)(2,1)} async-done(((bf16[512,1024]{1,0:T(8,128)(2,1)}), bf16[32,1024]{1,0:T(8,128)(2,1)}) %reduce-scatter.9.cloned.1.call-update) | async-done | bytes 65552 | tf_op jit(solution)/shard_map/reduce_scatter | solution.py:93
  362.4 1.5 convert_element_type.84
  363.9 73.6 %all-reduce.2.cloned.1.call-done = bf16[128,512]{1,0:T(8,128)(2,1)} async-done(((bf16[128,512]{1,0:T(8,128)(2,1)}), bf16[128,512]{1,0:T(8,128)(2,1)}) %all-reduce.2.cloned.1.call-update) | async-done | bytes 131088 | tf_op jit(solution)/shard_map/psum | solution.py:109
  437.5 1.6 convert_element_type.78
  (10 shorter events, 0.1 us)
Async XLA Ops:
  7.2 34.3 %copy-start = (bf16[512,1024]{1,0:T(8,128)(2,1)S(1)}, bf16[512,1024]{1,0:T(8,128)(2,1)}, u32[]{:S(2)}) copy-start(bf16[512,1024]{1,0:T(8,128)(2,1)} %param.11) | copy-start | bytes 3145732
  7.2 54.1 %all-gather.2.cloned.1.call-start = ((), (), s32[]{:S(2)}) async-start(), calls=%async_computation.4 | async-start | bytes 2228224 | tf_op jit(solution)/shard_map/all_gather | solution.py:62
  7.9 146.6 %reduce-scatter.7.cloned.1.call-start = ((), (), s32[]{:S(2)}) async-start(), calls=%async_computation.5 | async-start | bytes 2228224 | tf_op jit(solution)/shard_map/reduce_scatter | solution.py:101
  39.9 25.7 %copy-start.3 = (bf16[2048,64]{0,1:T(8,128)(2,1)}, bf16[2048,64]{0,1:T(8,128)(2,1)S(1)}, u32[]{:S(2)}) copy-start(bf16[2048,64]{0,1:T(8,128)(2,1)S(1)} %all_gather.9) | copy-start | bytes 786436
  65.6 2.2 copy-start.6
  65.6 2.2 copy-start.8
  67.8 12.0 %copy-start.2 = (f32[128,8,2048]{2,0,1:T(8,128)}, f32[128,8,2048]{2,0,1:T(8,128)S(1)}, u32[]{:S(2)}) copy-start(f32[128,8,2048]{2,0,1:T(8,128)S(1)} %get-tuple-element.30) | copy-start | bytes 25165828
  72.2 5.2 %copy-start.7 = (bf16[128,8,512]{0,2,1:T(8,128)(2,1)S(1)}, bf16[128,8,512]{0,2,1:T(8,128)(2,1)}, u32[]{:S(2)}) copy-start(bf16[128,8,512]{0,2,1:T(8,128)(2,1)} %fusion.18) | copy-start | bytes 3145732
  75.5 2.0 copy-start.1
  84.6 138.4 %reduce-scatter.13.cloned.1.call-start = ((), (), s32[]{:S(2)}) async-start(), calls=%async_computation.9 | async-start | bytes 557056
  88.7 204.0 %reduce-scatter.11.cloned.1.call-start = ((), (), s32[]{:S(2)}) async-start(), calls=%async_computation.8 | async-start | bytes 1114112 | tf_op jit(solution)/shard_map/reduce_scatter | solution.py:96
  98.8 263.6 %reduce-scatter.9.cloned.1.call-start = ((), (), s32[]{:S(2)}) async-start(), calls=%async_computation.7 | async-start | bytes 1114112 | tf_op jit(solution)/shard_map/reduce_scatter | solution.py:93
  105.9 3.6 copy-start.4
  108.2 329.3 %all-reduce.2.cloned.1.call-start = ((), (), s32[]{:S(2)}) async-start(), calls=%async_computation.6 | async-start | bytes 262144 | tf_op jit(solution)/shard_map/psum | solution.py:109
  109.4 45.1 %copy-start.5 = (bf16[128,8,128]{0,2,1:T(8,128)(2,1)S(1)}, bf16[128,8,128]{0,2,1:T(8,128)(2,1)}, u32[]{:S(2)}) copy-start(bf16[128,8,128]{0,2,1:T(8,128)(2,1)} %fusion.22) | copy-start | bytes 786436
Sparse Core Ops, SparseCore 0:
  10.4 50.8 all-gather.1
  84.7 69.7 reduce-scatter.6
  158.3 64.6 reduce-scatter.12
  226.7 65.9 reduce-scatter.10
  296.4 65.9 reduce-scatter.8
  364.7 72.7 all-reduce.1
where the time goes:
time: 447 us; the launch traced here: 446 us
  waiting for transfers between devices  305 us (68%)
  blocking collectives  60 us (13%)
  matrix products  43.2 us (10%)
  between operations  14.3 us (3%)
  local copies, waits for them, and re-layouts  13.3 us (3%)
  other arithmetic  10.3 us (2%)
    psum x1, waiting for transfers between devices, per_device(): lax.psum(partial_latent.astype(jnp.bfloat16), 'head').astype(jnp.float32)  73.6 us
    unnamed x7, waiting for transfers between devices  68.2 us
    reduce_scatter x1, waiting for transfers between devices, per_device(): lax.psum_scatter(weight_key_grad.astype(jnp.bfloat16), 'ctx', scatter_dim...  68.2 us
    dot_general x13, matrix products, product(): jnp.einsum(pattern, left_side, right_side, preferred_element_type=jnp.flo...  43.2 us
    reduce_scatter x1, waiting for transfers between devices, per_device(): lax.psum_scatter(all_latent.astype(jnp.bfloat16), 'ctx', scatter_dimensio...  41.4 us
    reduce_scatter x1, waiting for transfers between devices, per_device(): lax.psum_scatter(weight_value_grad.astype(jnp.bfloat16), 'ctx', scatter_d...  34.8 us
    psum x1, blocking collectives, per_device(): lax.psum(partial_rope.astype(jnp.bfloat16), 'head').astype(jnp.float32)  33.4 us
    all_gather x1, blocking collectives, per_device(): rope_piece = lax.all_gather(rope_key, 'ctx', axis=0, tiled=True)  26.6 us
  transfers between devices with their start and end apart: 6, of which 6 were waited for; matrix products, arithmetic and copies ran while one was open for 9% of the time, Pallas kernels for 0%

commit v1 on v0

--- a/solution.py
+++ b/solution.py
@@ -106,7 +106,7 @@
         ).astype(jnp.float32),
     )
     latent_grad, rope_grad = (
-        lax.psum(partial_latent.astype(jnp.bfloat16), "head").astype(jnp.float32),
+        lax.all_gather(partial_latent.astype(jnp.bfloat16), "head").sum(axis=0).astype(jnp.float32),
         lax.psum(partial_rope.astype(jnp.bfloat16), "head").astype(jnp.float32),
     )
     return (query_grad, latent_grad, rope_grad, up_key_grad, up_value_grad)

time: 447 us -> 411 us (0.919)
  waiting for transfers between devices: 305 us -> 269 us
    psum x1 -> x0, waiting for transfers between devices: 73.6 us -> none  [per_device(): lax.psum(partial_latent.astype(jnp.bfloat16), 'head').astype(jnp.float32)]
    all_gather x0 -> x1, waiting for transfers between devices: none -> 37.8 us  [per_device(): lax.all_gather(partial_latent.astype(jnp.bfloat16), 'head').sum(axis=0)]
    reduce_scatter x1, waiting for transfers between devices: 41.4 us -> 46.2 us  [per_device(): lax.psum_scatter(all_latent.astype(jnp.bfloat16), 'ctx', scatter_dimensio...]
  transfers between devices with their start and end apart: 6 -> 6, of which waited for: 6 -> 6; matrix products, arithmetic and copies ran while one was open for 9% -> 10% of each run, Pallas kernels for 0% -> 0%
where the time goes in v1:
time: 411 us
  waiting for transfers between devices  269 us (65%)
  blocking collectives  60 us (15%)
  matrix products  42.4 us (10%)
  between operations  14.3 us (3%)
  local copies, waits for them, and re-layouts  13.3 us (3%)
  other arithmetic  10.7 us (3%)
    reduce_scatter x1, waiting for transfers between devices, per_device(): lax.psum_scatter(weight_key_grad.astype(jnp.bfloat16), 'ctx', scatter_dim...  68.2 us
    unnamed x7, waiting for transfers between devices  64.3 us
    reduce_scatter x1, waiting for transfers between devices, per_device(): lax.psum_scatter(all_latent.astype(jnp.bfloat16), 'ctx', scatter_dimensio...  46.2 us
    dot_general x13, matrix products, product(): jnp.einsum(pattern, left_side, right_side, preferred_element_type=jnp.flo...  42.4 us
    all_gather x1, waiting for transfers between devices, per_device(): lax.all_gather(partial_latent.astype(jnp.bfloat16), 'head').sum(axis=0)  37.8 us
    reduce_scatter x1, waiting for transfers between devices, per_device(): lax.psum_scatter(weight_value_grad.astype(jnp.bfloat16), 'ctx', scatter_d...  34.8 us
    psum x1, blocking collectives, per_device(): lax.psum(partial_rope.astype(jnp.bfloat16), 'head').astype(jnp.float32)  33.4 us
    all_gather x1, blocking collectives, per_device(): rope_piece = lax.all_gather(rope_key, 'ctx', axis=0, tiled=True)  26.6 us
  transfers between devices with their start and end apart: 6, of which 6 were waited for; matrix products, arithmetic and copies ran while one was open for 10% of the time, Pallas kernels for 0%

profile of v1, /device:TPU:0, one launch (start us, length us, event | category | flops | bytes accessed | tf_op | source)
XLA Modules:
  0.0 410.7 jit_solution(9511381442061965321)
XLA Ops:
  7.2 0.0 copy-start
  7.2 0.0 all-gather.4.cloned.1.call-start
  7.2 0.7 all-gather.4.cloned.1.call-update
  7.9 0.0 reduce-scatter.7.cloned.1.call-start
  8.0 1.2 copy.63
  9.2 1.5 copy.90
  10.7 1.1 copy.91
  11.9 0.7 select_reduce_fusion.2
  12.6 0.8 select_reduce_fusion.1
  13.4 26.6 %all_gather.15 = bf16[2048,64]{0,1:T(8,128)(2,1)S(1)} all-gather(bf16[128,64]{0,1:T(8,128)(2,1)} %param.9), channel_id=1, replica_groups=mesh['ctx'=16,'head'=8] {'ctx'}, dimensions={0}, use_global_device_ids=true | all-gather | bytes 278528 | tf_op jit(solution)/shard_map/all_gather | solution.py:63
  40.0 1.5 fusion.18
  41.5 0.0 copy-done
  41.5 1.5 fusion.19
  42.9 0.2 broadcast_compare_fusion
  43.2 18.1 %all-gather.4.cloned.1.call-done = bf16[2048,512]{1,0:T(8,128)(2,1)} async-done(((bf16[128,512]{1,0:T(8,128)(2,1)}), bf16[2048,512]{1,0:T(8,128)(2,1)}) %all-gather.4.cloned.1.call-update) | async-done | bytes 2097168 | tf_op jit(solution)/shard_map/all_gather | solution.py:62
  61.3 4.3 %fusion.10 = f32[128,8,2048]{2,0,1:T(8,128)S(1)} fusion(bf16[128,8,512]{0,2,1:T(8,128)(2,1)} %fusion.18, bf16[2048,512]{1,0:T(8,128)(2,1)} %all-gather.4.cloned.1.call-done), kind=kOutput, calls=%fused_computation.18 | convolution fusion | flops 2147483648 | bytes 11534336 | tf_op jit(solution)/shard_map/thk,nk->thn/dot_general | solution.py:14
  65.6 0.0 copy-done.3
  65.6 0.0 copy-start.5
  65.6 0.0 copy-start.7
  65.6 2.2 select_reduce_fusion
  67.8 0.0 copy-start.2
  67.9 0.0 copy-done.5
  67.9 0.0 copy-done.7
  67.9 4.3 %fusion = (f32[128,8]{0,1:T(8,128)S(1)}, f32[128,8]{0,1:T(8,128)S(1)}, f32[128,8,2048]{2,0,1:T(8,128)S(1)}) fusion(f32[128,8,2048]{2,0,1:T(8,128)S(1)} %get-tuple-element.30, f32[128,8]{0,1:T(8,128)S(1)} %broadcast_maximum_fusion, pred[128,2048]{1,0:T(8,128)(4,1)S(1)} %broadcast_compare_fusion, bf16[128,8,512]{0,2,1:T(8,128)(2,1)S(1)} %copy-done.5, ...), kind=kOutput, calls=%fused_computation.6 | convolution fusion | flops 2157967360 | bytes 20197376 | tf_op jit(solution)/shard_map/thk,nk->thn/dot_general | solution.py:14
  72.2 0.0 copy-start.6
  72.2 3.2 multiply_convert_fusion
  75.5 0.0 copy-start.1
  75.5 2.0 copy-done.1
  77.4 0.0 copy-done.6
  77.4 2.4 fusion.46
  79.9 0.0 copy-done.2
  79.9 4.7 %fusion.2 = bf16[2048,512]{1,0:T(8,128)(2,1)} fusion(f32[2048,512,1]{1,0,2:T(8,128)S(1)} %fusion.46, bf16[128,8,512]{0,2,1:T(8,128)(2,1)S(1)} %copy-done.5, f32[128,8,2048]{2,0,1:T(8,128)S(1)} %get-tuple-element.30, f32[128,8]{0,1:T(8,128)S(1)} %get-tuple-element.27, pred[128,2048]{1,0:T(8,128)(4,1)S(1)} %broadcast_compare_fusion), kind=kOutput, calls=%fused_computation.9 | convolution fusion | flops 2155872256 | bytes 15994880 | tf_op jit(solution)/shard_map/thn,thk->nk/dot_general | solution.py:14
  84.5 0.0 reduce-scatter.7.cloned.1.call-update
  84.6 0.0 reduce-scatter.13.cloned.1.call-start
  84.6 3.0 fusion.3
  87.7 1.0 copy.87
  88.7 0.0 reduce-scatter.13.cloned.1.call-update
  88.7 0.0 reduce-scatter.11.cloned.1.call-start
  88.8 7.7 %convolution_convert_fusion.1 = bf16[8,512,128]{1,2,0:T(8,128)(2,1)} fusion(bf16[128,8,128]{0,2,1:T(8,128)(2,1)S(1)} %bitcast.82, bf16[2048,512]{1,0:T(8,128)(2,1)} %all-gather.4.cloned.1.call-done, f32[128,8,2048]{2,0,1:T(8,128)} %copy-done.2, f32[128,8]{0,1:T(8,128)S(1)} %get-tuple-element.27, pred[128,2048]{1,0:T(8,128)(4,1)S(1)} %broadcast_compare_fusion), kind=kOutput, calls=%fused_computation.21 | convolution fusion | flops 2289041408 | bytes 12062720 | tf_op jit(solution)/shard_map/thk,thd->khd/dot_general | solution.py:14
  96.5 2.3 copy.78
  98.8 0.0 reduce-scatter.11.cloned.1.call-update
  98.8 0.3 reduce-scatter.9.cloned.1.call-start
  99.1 5.4 %fusion.12 = bf16[128,8,512]{2,0,1:T(8,128)(2,1)S(1)} fusion(bf16[128,8,2048]{2,0,1:T(8,128)(2,1)} %copy-done.1, bf16[2048,512]{1,0:T(8,128)(2,1)} %all-gather.4.cloned.1.call-done), kind=kOutput, calls=%fused_computation.24 | convolution fusion | flops 2148007936 | bytes 7340032 | tf_op jit(solution)/shard_map/thn,nk->thk/dot_general | solution.py:14
  104.5 1.4 convolution_convert_fusion
  105.9 2.4 copy.76
  108.2 0.0 reduce-scatter.9.cloned.1.call-update
  108.3 0.0 all-gather.6.cloned.1.call-start
  108.3 46.2 %reduce-scatter.7.cloned.1.call-done = bf16[128,512]{1,0:T(8,128)(2,1)} async-done(((bf16[2048,512]{1,0:T(8,128)(2,1)}), bf16[128,512]{1,0:T(8,128)(2,1)}) %reduce-scatter.7.cloned.1.call-update) | async-done | bytes 131088 | tf_op jit(solution)/shard_map/reduce_scatter | solution.py:101
  154.5 0.0 all-gather.6.cloned.1.call-update
  154.5 0.4 fusion.22
  155.0 0.0 copy-done.4
  155.0 3.6 convolution_convert_fusion.5
  158.6 0.9 copy.79
  159.5 63.5 %reduce-scatter.13.cloned.1.call-done = bf16[128,64]{1,0:T(8,128)(2,1)} async-done(((bf16[2048,64]{1,0:T(8,128)(2,1)}), bf16[128,64]{1,0:T(8,128)(2,1)}) %reduce-scatter.13.cloned.1.call-update) | async-done | bytes 16400
  223.1 0.8 copy.88
  223.9 33.4 %psum.7 = bf16[128,64]{0,1:T(8,128)(2,1)S(1)} all-reduce(bf16[128,64]{0,1:T(8,128)(2,1)S(1)} %copy.88), channel_id=1, replica_groups=mesh['ctx'=16,'head'=8] {'head'}, use_global_device_ids=true, to_apply=%region_8.9 | all-reduce | flops 8192 | bytes 32768 | tf_op jit(solution)/shard_map/psum | solution.py:110
  257.3 0.6 convert_element_type.82
  257.9 34.8 %reduce-scatter.11.cloned.1.call-done = bf16[32,1024]{1,0:T(8,128)(2,1)} async-done(((bf16[512,1024]{1,0:T(8,128)(2,1)}), bf16[32,1024]{1,0:T(8,128)(2,1)}) %reduce-scatter.11.cloned.1.call-update) | async-done | bytes 65552 | tf_op jit(solution)/shard_map/reduce_scatter | solution.py:96
  292.7 1.5 convert_element_type.91
  294.2 68.2 %reduce-scatter.9.cloned.1.call-done = bf16[32,1024]{1,0:T(8,128)(2,1)} async-done(((bf16[512,1024]{1,0:T(8,128)(2,1)}), bf16[32,1024]{1,0:T(8,128)(2,1)}) %reduce-scatter.9.cloned.1.call-update) | async-done | bytes 65552 | tf_op jit(solution)/shard_map/reduce_scatter | solution.py:93
  362.4 1.5 convert_element_type.86
  363.9 37.8 %all-gather.6.cloned.1.call-done = bf16[1024,512]{1,0:T(8,128)(2,1)} async-done(((bf16[128,512]{1,0:T(8,128)(2,1)}), bf16[1024,512]{1,0:T(8,128)(2,1)}) %all-gather.6.cloned.1.call-update) | async-done | bytes 1048592 | tf_op jit(solution)/shard_map/all_gather | solution.py:109
  401.7 1.4 reduce_sum.56
  403.1 0.7 convert_element_type.80
  (9 shorter events, 0.1 us)
Async XLA Ops:
  7.2 34.3 %copy-start = (bf16[512,1024]{1,0:T(8,128)(2,1)S(1)}, bf16[512,1024]{1,0:T(8,128)(2,1)}, u32[]{:S(2)}) copy-start(bf16[512,1024]{1,0:T(8,128)(2,1)} %param.11) | copy-start | bytes 3145732
  7.2 54.1 %all-gather.4.cloned.1.call-start = ((), (), s32[]{:S(2)}) async-start(), calls=%async_computation.4 | async-start | bytes 2228224 | tf_op jit(solution)/shard_map/all_gather | solution.py:62
  7.9 146.6 %reduce-scatter.7.cloned.1.call-start = ((), (), s32[]{:S(2)}) async-start(), calls=%async_computation.5 | async-start | bytes 2228224 | tf_op jit(solution)/shard_map/reduce_scatter | solution.py:101
  39.9 25.7 %copy-start.3 = (bf16[2048,64]{0,1:T(8,128)(2,1)}, bf16[2048,64]{0,1:T(8,128)(2,1)S(1)}, u32[]{:S(2)}) copy-start(bf16[2048,64]{0,1:T(8,128)(2,1)S(1)} %all_gather.15) | copy-start | bytes 786436
  65.6 2.2 copy-start.5
  65.6 2.2 copy-start.7
  67.8 12.0 %copy-start.2 = (f32[128,8,2048]{2,0,1:T(8,128)}, f32[128,8,2048]{2,0,1:T(8,128)S(1)}, u32[]{:S(2)}) copy-start(f32[128,8,2048]{2,0,1:T(8,128)S(1)} %get-tuple-element.30) | copy-start | bytes 25165828
  72.2 5.2 %copy-start.6 = (bf16[128,8,512]{0,2,1:T(8,128)(2,1)S(1)}, bf16[128,8,512]{0,2,1:T(8,128)(2,1)}, u32[]{:S(2)}) copy-start(bf16[128,8,512]{0,2,1:T(8,128)(2,1)} %fusion.18) | copy-start | bytes 3145732
  75.5 2.0 copy-start.1
  84.6 138.5 %reduce-scatter.13.cloned.1.call-start = ((), (), s32[]{:S(2)}) async-start(), calls=%async_computation.9 | async-start | bytes 557056
  88.7 204.0 %reduce-scatter.11.cloned.1.call-start = ((), (), s32[]{:S(2)}) async-start(), calls=%async_computation.7 | async-start | bytes 1114112 | tf_op jit(solution)/shard_map/reduce_scatter | solution.py:96
  98.8 263.6 %reduce-scatter.9.cloned.1.call-start = ((), (), s32[]{:S(2)}) async-start(), calls=%async_computation.6 | async-start | bytes 1114112 | tf_op jit(solution)/shard_map/reduce_scatter | solution.py:93
  105.9 49.1 %copy-start.4 = (bf16[2048,64]{0,1:T(8,128)(2,1)S(1)}, bf16[2048,64]{0,1:T(8,128)(2,1)}, u32[]{:S(2)}) copy-start(bf16[2048,64]{0,1:T(8,128)(2,1)} %copy-done.3) | copy-start | bytes 786436
  108.3 293.5 %all-gather.6.cloned.1.call-start = ((), (), s32[]{:S(2)}) async-start(), calls=%async_computation.8 | async-start | bytes 1179648 | tf_op jit(solution)/shard_map/all_gather | solution.py:109
Sparse Core Ops, SparseCore 0:
  10.4 50.8 all-gather.3
  84.7 69.7 reduce-scatter.6
  158.3 64.7 reduce-scatter.12
  226.7 65.9 reduce-scatter.10
  296.4 65.9 reduce-scatter.8
  363.9 37.7 all-gather.5
